TPU v7x, 512 devices: a whole 4x4x16 slice. The times are simulated.
512 devices in a mesh: gx: 64 (over x, y, z_lo), gy: 8 (over z_hi, core).
Axes of the slice: x: 4, y: 4, z: 16 (z_hi: 4, z_lo: 4; z = z_hi * 4 + z_lo), core: 2. Of those that a mesh axis runs over, the one named last changes fastest.
Arguments:
- displacement: float32 [3, 1536, 192, 128], P(None, 'gx', 'gy'), may hold values from -25 to 25
- velocity: float32 [3, 1536, 192, 128], P(None, 'gx', 'gy'), may hold values from -6 to 6
- history: float32 [1536, 192, 128], P('gx', 'gy'), may hold values from 1 to 10
- zone: int32 [1536, 192, 128], P('gx', 'gy'), may hold values from 0 to 7
- zone_modulus: float32 [8], replicated, may hold values from 0.5 to 2
- zone_threshold: float32 [8], replicated, may hold values from 0.5 to 4
- zone_density: float32 [8], replicated, may hold values from 0.5 to 2
Outputs:
- new_displacement: float32 [3, 1536, 192, 128], P(None, 'gx', 'gy')
- new_velocity: float32 [3, 1536, 192, 128], P(None, 'gx', 'gy')
- new_history: float32 [1536, 192, 128], P('gx', 'gy')
All inputs are finite; a program needn't handle non-finite values.
Results may differ from a plain program's by a relative error of at most 0.000068.
Values sent between devices are 32-bit elements; how exact they have to be, the bound alone decides.
A program may use at most 64 MiB of HBM per device.

v0:
```python
import jax
import jax.numpy as jnp
from jax import lax
from jax.sharding import PartitionSpec as P

RADIUS = 24


time_step = 0.1
softening = 0.5


def passed_along(shard, axis, by):
    peers = lax.axis_size(axis)
    pairs = [(i, i + by) for i in range(peers) if 0 <= i + by < peers]
    return lax.ppermute(shard, axis, pairs)


def padded(block, sides, width):
    for axis, dim in sides:
        count = lax.axis_size(axis)
        forward = [(i, i + 1) for i in range(count - 1)]
        backward = [(target, source) for source, target in forward]
        low = lax.ppermute(
            lax.slice_in_dim(block, block.shape[dim] - width, None, axis=dim), axis, forward
        )
        high = lax.ppermute(lax.slice_in_dim(block, 0, width, axis=dim), axis, backward)
        block = jnp.concatenate([low, block, high], axis=dim)
    return block


def band_weight(offset):
    ratio = offset.astype(jnp.float32) / RADIUS
    return jnp.where(jnp.abs(offset) <= RADIUS, 1.0 - 0.5 * ratio * ratio, 0.0)


def local_band(nrows, ncols, first):
    left = lax.broadcasted_iota(jnp.int32, (nrows, ncols), 0)
    right = lax.broadcasted_iota(jnp.int32, (nrows, ncols), 1)
    return band_weight(right + first - left)


def coverage(start, count, total):
    place = start + lax.broadcasted_iota(jnp.int32, (count, 2 * RADIUS + 1), 0)
    offset = lax.broadcasted_iota(jnp.int32, (count, 2 * RADIUS + 1), 1) - RADIUS
    inside = (place + offset >= 0) & (place + offset < total)
    return jnp.sum(jnp.where(inside, band_weight(offset), 0.0), axis=1)


def lookup(zone, table):
    result = jnp.zeros(zone.shape, jnp.float32)
    for level in range(table.shape[0]):
        result = jnp.where(zone == level, table[level], result)
    return result


def pass_rows(block, count):
    weights = local_band(count, block.shape[0], -RADIUS)
    return jnp.einsum("ab,byz->ayz", weights, block, precision=lax.Precision.HIGHEST)


def pass_cols(block, count):
    weights = local_band(count, block.shape[1], -RADIUS)
    return jnp.einsum("ab,xbz->xaz", weights, block, precision=lax.Precision.HIGHEST)


def body(displacement, velocity, history, zone, zone_modulus, zone_threshold, zone_density):
    nrows, ncols, depth = history.shape
    front_x = passed_along(displacement[:, 0:1], "gx", -1)
    front_y = passed_along(displacement[:, :, 0:1], "gy", -1)
    ahead_x = jnp.concatenate([displacement[:, 1:], front_x], axis=1)
    ahead_y = jnp.concatenate([displacement[:, :, 1:], front_y], axis=2)
    ahead_z = jnp.concatenate(
        [displacement[:, :, :, 1:], jnp.zeros_like(displacement[:, :, :, 0:1])], axis=3
    )
    grads = [ahead_x - displacement, ahead_y - displacement, ahead_z - displacement]
    strain = [[0.5 * (grads[i][j] + grads[j][i]) for j in range(3)] for i in range(3)]
    squares = strain[0][0] ** 2 + strain[1][1] ** 2 + strain[2][2] ** 2
    squares = squares + 2.0 * (strain[0][1] ** 2 + strain[0][2] ** 2 + strain[1][2] ** 2)
    equivalent = jnp.sqrt(squares)
    depth_band = local_band(depth, depth, 0)
    along_z = jnp.dot(
        equivalent.reshape(-1, depth), depth_band, precision=lax.Precision.HIGHEST
    ).reshape(nrows, ncols, depth)
    wide = padded(along_z, (("gx", 0),), RADIUS)
    middle = pass_rows(wide, nrows)
    tall = padded(middle, (("gy", 1),), RADIUS)
    smoothed = pass_cols(tall, ncols)
    cover_x = coverage(lax.axis_index("gx") * nrows, nrows, nrows * lax.axis_size("gx"))
    cover_y = coverage(lax.axis_index("gy") * ncols, ncols, ncols * lax.axis_size("gy"))
    cover_z = coverage(0, depth, depth)
    average = smoothed / (cover_x[:, None, None] * cover_y[None, :, None] * cover_z[None, None, :])
    new_history = jnp.maximum(history, average)
    modulus = lookup(zone, zone_modulus)
    threshold = lookup(zone, zone_threshold)
    density = lookup(zone, zone_density)
    bounded = jnp.maximum(new_history, threshold)
    damage = 1.0 - threshold / bounded * jnp.exp(-softening * (bounded - threshold))
    trace = strain[0][0] + strain[1][1] + strain[2][2]
    intact = 1.0 - damage
    stress = [
        [
            intact * ((modulus * trace if i == j else 0.0) + 2.0 * modulus * strain[i][j])
            for j in range(3)
        ]
        for i in range(3)
    ]
    last_x = jnp.stack([stress[0][j][-1:] for j in range(3)])
    last_y = jnp.stack([stress[1][j][:, -1:] for j in range(3)])
    back_x = passed_along(last_x, "gx", 1)
    back_y = passed_along(last_y, "gy", 1)
    force = []
    for j in range(3):
        before_x = jnp.concatenate([back_x[j], stress[0][j][:-1]], axis=0)
        before_y = jnp.concatenate([back_y[j], stress[1][j][:, :-1]], axis=1)
        before_z = jnp.concatenate(
            [jnp.zeros_like(stress[2][j][:, :, 0:1]), stress[2][j][:, :, :-1]], axis=2
        )
        total = stress[0][j] - before_x + (stress[1][j] - before_y) + (stress[2][j] - before_z)
        force.append(total)
    new_velocity = velocity + time_step * jnp.stack(force) / density[None]
    new_displacement = displacement + time_step * new_velocity
    return (new_displacement, new_velocity, new_history)


def solution(mesh):
    return jax.shard_map(
        body,
        mesh=mesh,
        in_specs=(
            P(None, "gx", "gy", None),
            P(None, "gx", "gy", None),
            P("gx", "gy", None),
            P("gx", "gy", None),
            P(),
            P(),
            P(),
        ),
        out_specs=(P(None, "gx", "gy", None), P(None, "gx", "gy", None), P("gx", "gy", None)),
        check_vma=False,
    )
```

profile of v0, /device:TPU:7, one launch (start us, length us, event | category | flops | bytes accessed | tf_op | source)
XLA Modules:
  0.0 95.6 jit_solution(10000175798980577702)
XLA Ops:
  0.6 0.8 slice.195
  1.4 9.0 %collective-permute-start = (f32[3,1,24,128]{3,2,1,0:T(8,128)S(1)}, f32[3,1,24,128]{3,2,1,0:T(8,128)S(1)}, u32[]{:S(2)}, u32[]{:S(2)}) collective-permute-start(f32[3,1,24,128]{3,2,1,0:T(8,128)S(1)} %slice.195), channel_id=1, source_target_pairs={{8,0},{16,8},{24,16},{32,24},{40,32},{48,40},{56,48},{64,56},{72,6... | collective-permute-start | bytes 110600 | tf_op jit(solution)/shard_map/ppermute | solution.py:16
  10.4 1.0 %slice.198 = f32[3,24,1,128]{3,2,1,0:T(1,128)S(1)} slice(f32[3,24,24,128]{3,2,1,0:T(8,128)} %param.7), slice={[0:3], [0:24], [0:1], [0:128]} | slice | bytes 73728 | tf_op jit(solution)/shard_map/slice | solution.py:70
  11.4 2.9 %collective-permute-start.1 = (f32[3,24,1,128]{3,2,1,0:T(1,128)S(1)}, f32[3,24,1,128]{3,2,1,0:T(1,128)S(1)}, u32[]{:S(2)}, u32[]{:S(2)}) collective-permute-start(f32[3,24,1,128]{3,2,1,0:T(1,128)S(1)} %slice.198), channel_id=1, source_target_pairs={{1,0},{2,1},{3,2},{4,3},{5,4},{6,5},{7,6},{9,8},{10,9},{11,10},{12... | collective-permute-start | bytes 110600 | tf_op jit(solution)/shard_map/ppermute | solution.py:16
  14.3 0.6 copy-done.3
  14.9 0.7 fusion.113
  15.7 0.2 fusion.73
  15.9 0.5 copy-done.4
  16.4 0.7 fusion.111
  17.0 1.3 %slice.197 = f32[3,24,23,128]{3,2,1,0:T(8,128)S(1)} slice(f32[3,24,24,128]{3,2,1,0:T(8,128)} %param.7), slice={[0:3], [0:24], [1:24], [0:128]} | slice | bytes 1695744 | tf_op jit(solution)/shard_map/slice | solution.py:72
  18.5 0.3 slice.200
  18.8 3.9 %collective-permute-done.1 = f32[3,24,1,128]{3,2,1,0:T(1,128)S(1)} collective-permute-done((f32[3,24,1,128]{3,2,1,0:T(1,128)S(1)}, f32[3,24,1,128]{3,2,1,0:T(1,128)S(1)}, u32[]{:S(2)}, u32[]{:S(2)}) %collective-permute-start.1) | collective-permute-done | bytes 36896 | tf_op jit(solution)/shard_map/ppermute | solution.py:16
  22.7 0.3 maximum_subtract_fusion
  23.0 0.7 fusion.33
  23.7 1.9 %collective-permute-start.2 = (f32[24,24,128]{2,1,0:T(8,128)S(1)}, f32[24,24,128]{2,1,0:T(8,128)S(1)}, u32[]{:S(2)}, u32[]{:S(2)}) collective-permute-start(f32[24,24,128]{2,1,0:T(8,128)S(1)} %fusion.33), channel_id=1, source_target_pairs={{0,8},{8,16},{16,24},{24,32},{32,40},{40,48},{48,56},{56,64},{64,7... | collective-permute-start | bytes 884744 | tf_op jit(solution)/shard_map/ppermute | solution.py:24
  25.6 8.2 %collective-permute-start.3 = (f32[24,24,128]{2,1,0:T(8,128)S(1)}, f32[24,24,128]{2,1,0:T(8,128)S(1)}, u32[]{:S(2)}, u32[]{:S(2)}) collective-permute-start(f32[24,24,128]{2,1,0:T(8,128)S(1)} %fusion.33), channel_id=1, source_target_pairs={{8,0},{16,8},{24,16},{32,24},{40,32},{48,40},{56,48},{64,56},{72,6... | collective-permute-start | bytes 884744 | tf_op jit(solution)/shard_map/ppermute | solution.py:27
  33.9 5.2 %collective-permute-done.2 = f32[24,24,128]{2,1,0:T(8,128)S(1)} collective-permute-done((f32[24,24,128]{2,1,0:T(8,128)S(1)}, f32[24,24,128]{2,1,0:T(8,128)S(1)}, u32[]{:S(2)}, u32[]{:S(2)}) %collective-permute-start.2) | collective-permute-done | bytes 294944 | tf_op jit(solution)/shard_map/ppermute | solution.py:24
  39.2 0.6 fusion.5
  39.8 8.7 %collective-permute-start.4 = (f32[24,24,128]{2,0,1:T(8,128)S(1)}, f32[24,24,128]{2,0,1:T(8,128)S(1)}, u32[]{:S(2)}, u32[]{:S(2)}) collective-permute-start(f32[24,24,128]{2,0,1:T(8,128)S(1)} %fusion.5), channel_id=1, source_target_pairs={{0,1},{1,2},{2,3},{3,4},{4,5},{5,6},{6,7},{8,9},{9,10},{10,11},{11... | collective-permute-start | bytes 884744 | tf_op jit(solution)/shard_map/ppermute | solution.py:24
  48.6 1.9 %collective-permute-start.5 = (f32[24,24,128]{2,0,1:T(8,128)S(1)}, f32[24,24,128]{2,0,1:T(8,128)S(1)}, u32[]{:S(2)}, u32[]{:S(2)}) collective-permute-start(f32[24,24,128]{2,0,1:T(8,128)S(1)} %fusion.5), channel_id=1, source_target_pairs={{1,0},{2,1},{3,2},{4,3},{5,4},{6,5},{7,6},{9,8},{10,9},{11,10},{12... | collective-permute-start | bytes 884744 | tf_op jit(solution)/shard_map/ppermute | solution.py:27
  50.5 0.7 fusion.112
  51.2 5.5 %select_select_fusion = (f32[24,24,128]{2,1,0:T(8,128)S(1)}, pred[24,24,128]{2,1,0:T(8,128)(4,1)S(1)}, pred[24,24,128]{2,1,0:T(8,128)(4,1)S(1)}, pred[24,24,128]...) fusion(f32[]{:T(128)} %bitcast.50, f32[]{:T(128)} %bitcast.49, ...), kind=kLoop, calls=%fused_computation.55 | loop fusion | flops 1179648 | bytes 1179680 | tf_op jit(solution)/shard_map/jit(_where)/select_n | solution.py:53
  56.7 12.2 %collective-permute-done.5 = f32[24,24,128]{2,0,1:T(8,128)S(1)} collective-permute-done((f32[24,24,128]{2,0,1:T(8,128)S(1)}, f32[24,24,128]{2,0,1:T(8,128)S(1)}, u32[]{:S(2)}, u32[]{:S(2)}) %collective-permute-start.5) | collective-permute-done | bytes 294944 | tf_op jit(solution)/shard_map/ppermute | solution.py:27
  69.1 11.9 %add_multiply_fusion = (f32[24,24,128]{2,1,0:T(8,128)S(1)}, f32[24,24,128]{2,1,0:T(8,128)S(1)}, f32[24,24,128]{2,1,0:T(8,128)S(1)}, f32[24,24,128]{2,1,0:T(8,128)S(1)}, f32[24,24,128]{2,1,0:T(8,128)}) fusion(f32[3,24,24,128]{3,2,1,0:T(8,128)S(1)} %get-tuple-element.27, f32[3,24,24,128]{3,2,1,0:T(8,128)S(1)} %get-tuple-element.26, ...), kind=kOutput, calls=%fused_computation.56 | convolution fusion | flops 66591936 | bytes 4131936 | tf_op jit(solution)/shard_map/ab,xbz->xaz/dot_general | solution.py:64
  80.9 0.3 add_multiply_fusion.1
  81.3 1.9 %collective-permute-start.7 = (f32[3,24,1,128]{3,1,2,0:T(8,128)S(1)}, f32[3,24,1,128]{3,1,2,0:T(8,128)S(1)}, u32[]{:S(2)}, u32[]{:S(2)}) collective-permute-start(f32[3,24,1,128]{3,1,2,0:T(8,128)S(1)} %pad_maximum_fusion.3), channel_id=1, source_target_pairs={{0,1},{1,2},{2,3},{3,4},{4,5},{5,6},{6,7},{8,9},{9,10},{10,11},{11... | collective-permute-start | bytes 110600 | tf_op jit(solution)/shard_map/ppermute | solution.py:16
  83.3 1.9 %collective-permute-start.6 = (f32[3,1,24,128]{3,2,1,0:T(8,128)S(1)}, f32[3,1,24,128]{3,2,1,0:T(8,128)S(1)}, u32[]{:S(2)}, u32[]{:S(2)}) collective-permute-start(f32[3,1,24,128]{3,2,1,0:T(8,128)S(1)} %pad_maximum_fusion.2), channel_id=1, source_target_pairs={{0,8},{8,16},{16,24},{24,32},{32,40},{40,48},{48,56},{56,64},{64,7... | collective-permute-start | bytes 110600 | tf_op jit(solution)/shard_map/ppermute | solution.py:16
  85.3 7.6 %collective-permute-done.6 = f32[3,1,24,128]{3,2,1,0:T(8,128)S(1)} collective-permute-done((f32[3,1,24,128]{3,2,1,0:T(8,128)S(1)}, f32[3,1,24,128]{3,2,1,0:T(8,128)S(1)}, u32[]{:S(2)}, u32[]{:S(2)}) %collective-permute-start.6) | collective-permute-done | bytes 36896 | tf_op jit(solution)/shard_map/ppermute | solution.py:16
  92.9 0.2 fusion.29
  93.0 0.3 fusion.26
  93.4 0.8 copy-done.1
  94.2 1.4 %multiply_add_fusion = (f32[3,24,24,128]{3,2,1,0:T(8,128)}, f32[3,24,24,128]{3,2,1,0:T(8,128)}) fusion(f32[3,24,24,128]{3,2,1,0:T(8,128)S(1)} %copy-done, f32[3,24,24,128]{3,2,1,0:T(8,128)S(1)} %copy-done.1, f32[24,24,128]{2,1,0:T(8,128)S(1)} %get-tuple-element.7, f32[1,24,24,128]{3,2,1,0:T(8,128)S(1)} %get-tuple-element.29, ...), kind=kLoop, calls=%fused_computation.13 | loop fusion | flops 1548288 | bytes 4718592 | tf_op jit(solution)/shard_map/add | solution.py:122
  (39 shorter events, 0.6 us)
Async XLA Ops:
  1.4 17.4 %collective-permute-start = (f32[3,1,24,128]{3,2,1,0:T(8,128)S(1)}, f32[3,1,24,128]{3,2,1,0:T(8,128)S(1)}, u32[]{:S(2)}, u32[]{:S(2)}) collective-permute-start(f32[3,1,24,128]{3,2,1,0:T(8,128)S(1)} %slice.195), channel_id=1, source_target_pairs={{8,0},{16,8},{24,16},{32,24},{40,32},{48,40},{56,48},{64,56},{72,6... | collective-permute-start | bytes 110600 | tf_op jit(solution)/shard_map/ppermute | solution.py:16
  11.4 11.3 %collective-permute-start.1 = (f32[3,24,1,128]{3,2,1,0:T(1,128)S(1)}, f32[3,24,1,128]{3,2,1,0:T(1,128)S(1)}, u32[]{:S(2)}, u32[]{:S(2)}) collective-permute-start(f32[3,24,1,128]{3,2,1,0:T(1,128)S(1)} %slice.198), channel_id=1, source_target_pairs={{1,0},{2,1},{3,2},{4,3},{5,4},{6,5},{7,6},{9,8},{10,9},{11,10},{12... | collective-permute-start | bytes 110600 | tf_op jit(solution)/shard_map/ppermute | solution.py:16
  14.3 0.7 copy-start.3
  15.7 0.7 copy-start.4
  17.0 1.4 %copy-start = (f32[3,24,24,128]{3,2,1,0:T(8,128)S(1)}, f32[3,24,24,128]{3,2,1,0:T(8,128)}, u32[]{:S(2)}) copy-start(f32[3,24,24,128]{3,2,1,0:T(8,128)} %param.7) | copy-start | bytes 2654212
  18.8 3.9 %slice-start = ((f32[3,24,24,128]{3,2,1,0:T(8,128)}), f32[3,23,24,128]{3,2,1,0:T(8,128)S(1)}, s32[]{:S(2)}) async-start(f32[3,24,24,128]{3,2,1,0:T(8,128)} %param.7), calls=%async_computation | async-start | bytes 1695744 | tf_op jit(solution)/shard_map/slice | solution.py:71
  23.7 15.4 %collective-permute-start.2 = (f32[24,24,128]{2,1,0:T(8,128)S(1)}, f32[24,24,128]{2,1,0:T(8,128)S(1)}, u32[]{:S(2)}, u32[]{:S(2)}) collective-permute-start(f32[24,24,128]{2,1,0:T(8,128)S(1)} %fusion.33), channel_id=1, source_target_pairs={{0,8},{8,16},{16,24},{24,32},{32,40},{40,48},{48,56},{56,64},{64,7... | collective-permute-start | bytes 884744 | tf_op jit(solution)/shard_map/ppermute | solution.py:24
  25.6 13.5 %collective-permute-start.3 = (f32[24,24,128]{2,1,0:T(8,128)S(1)}, f32[24,24,128]{2,1,0:T(8,128)S(1)}, u32[]{:S(2)}, u32[]{:S(2)}) collective-permute-start(f32[24,24,128]{2,1,0:T(8,128)S(1)} %fusion.33), channel_id=1, source_target_pairs={{8,0},{16,8},{24,16},{32,24},{40,32},{48,40},{56,48},{64,56},{72,6... | collective-permute-start | bytes 884744 | tf_op jit(solution)/shard_map/ppermute | solution.py:27
  39.2 11.3 %copy-start.5 = (f32[8]{0:T(128)S(1)}, f32[8]{0:T(128)}, u32[]{:S(2)}) copy-start(f32[8]{0:T(128)} %param.11) | copy-start | bytes 100
  39.2 12.0 %copy-start.2 = (s32[24,24,128]{2,1,0:T(8,128)S(1)}, s32[24,24,128]{2,1,0:T(8,128)}, u32[]{:S(2)}) copy-start(s32[24,24,128]{2,1,0:T(8,128)} %param.10) | copy-start | bytes 884740
  39.8 16.9 %collective-permute-start.4 = (f32[24,24,128]{2,0,1:T(8,128)S(1)}, f32[24,24,128]{2,0,1:T(8,128)S(1)}, u32[]{:S(2)}, u32[]{:S(2)}) collective-permute-start(f32[24,24,128]{2,0,1:T(8,128)S(1)} %fusion.5), channel_id=1, source_target_pairs={{0,1},{1,2},{2,3},{3,4},{4,5},{5,6},{6,7},{8,9},{9,10},{10,11},{11... | collective-permute-start | bytes 884744 | tf_op jit(solution)/shard_map/ppermute | solution.py:24
  48.6 20.4 %collective-permute-start.5 = (f32[24,24,128]{2,0,1:T(8,128)S(1)}, f32[24,24,128]{2,0,1:T(8,128)S(1)}, u32[]{:S(2)}, u32[]{:S(2)}) collective-permute-start(f32[24,24,128]{2,0,1:T(8,128)S(1)} %fusion.5), channel_id=1, source_target_pairs={{1,0},{2,1},{3,2},{4,3},{5,4},{6,5},{7,6},{9,8},{10,9},{11,10},{12... | collective-permute-start | bytes 884744 | tf_op jit(solution)/shard_map/ppermute | solution.py:27
  56.7 12.3 %copy-start.6 = (f32[24,24,128]{2,1,0:T(8,128)S(1)}, f32[24,24,128]{2,1,0:T(8,128)}, u32[]{:S(2)}) copy-start(f32[24,24,128]{2,1,0:T(8,128)} %param.9) | copy-start | bytes 884740
  81.3 4.0 %collective-permute-start.7 = (f32[3,24,1,128]{3,1,2,0:T(8,128)S(1)}, f32[3,24,1,128]{3,1,2,0:T(8,128)S(1)}, u32[]{:S(2)}, u32[]{:S(2)}) collective-permute-start(f32[3,24,1,128]{3,1,2,0:T(8,128)S(1)} %pad_maximum_fusion.3), channel_id=1, source_target_pairs={{0,1},{1,2},{2,3},{3,4},{4,5},{5,6},{6,7},{8,9},{9,10},{10,11},{11... | collective-permute-start | bytes 110600 | tf_op jit(solution)/shard_map/ppermute | solution.py:16
  83.3 9.5 %collective-permute-start.6 = (f32[3,1,24,128]{3,2,1,0:T(8,128)S(1)}, f32[3,1,24,128]{3,2,1,0:T(8,128)S(1)}, u32[]{:S(2)}, u32[]{:S(2)}) collective-permute-start(f32[3,1,24,128]{3,2,1,0:T(8,128)S(1)} %pad_maximum_fusion.2), channel_id=1, source_target_pairs={{0,8},{8,16},{16,24},{24,32},{32,40},{40,48},{48,56},{56,64},{64,7... | collective-permute-start | bytes 110600 | tf_op jit(solution)/shard_map/ppermute | solution.py:16
  93.0 1.2 %copy-start.1 = (f32[3,24,24,128]{3,2,1,0:T(8,128)S(1)}, f32[3,24,24,128]{3,2,1,0:T(8,128)}, u32[]{:S(2)}) copy-start(f32[3,24,24,128]{3,2,1,0:T(8,128)} %param.8) | copy-start | bytes 2654212
where the time goes:
time: 97.3 us; the launch traced here: 95.6 us
  starting transfers between devices  36.4 us (37%)
  waiting for transfers between devices  28.9 us (30%)
  matrix products  13.2 us (14%)
  other arithmetic  8.51 us (9%)
  local copies, waits for them, and re-layouts  7.62 us (8%)
    ppermute x4, starting transfers between devices, passed_along(): return lax.ppermute(shard, axis, pairs)  15.7 us
    ppermute x2, waiting for transfers between devices, padded(): lax.ppermute(lax.slice_in_dim(block, 0, width, axis=dim), axis, backward)  12.2 us
    dot_general x1, matrix products, pass_cols(): jnp.einsum('ab,xbz->xaz', weights, block, precision=lax.Precision.HIGHEST)  11.9 us
    ppermute x4, waiting for transfers between devices, passed_along(): return lax.ppermute(shard, axis, pairs)  11.4 us
    ppermute x2, starting transfers between devices, padded(): lax.ppermute(lax.slice_in_dim(block, block.shape[dim] - width, None, axis...  10.6 us
    ppermute x2, starting transfers between devices, padded(): lax.ppermute(lax.slice_in_dim(block, 0, width, axis=dim), axis, backward)  10.1 us
    select_n x1, other arithmetic, lookup(): result = jnp.where(zone == level, table[level], result)  5.51 us
    ppermute x2, waiting for transfers between devices, padded(): lax.ppermute(lax.slice_in_dim(block, block.shape[dim] - width, None, axis...  5.25 us
  transfers between devices with their start and end apart: 8, of which 4 were waited for; matrix products, arithmetic and copies ran while one was open for 11% of the time, Pallas kernels for 0%

commit v1 on v0

v1 whole, which is shorter than its diff:
```python
import functools

import jax
import jax.numpy as jnp
from jax import lax
from jax.experimental import pallas as pl
from jax.experimental.pallas import tpu as pltpu
from jax.sharding import PartitionSpec as P

RADIUS = 24
TAPS = 2 * RADIUS + 1
N = 24
DEPTH = 128
CH = 8
F32 = jnp.float32
MESH = pl.DeviceIdType.MESH
HIGHEST = lax.Precision.HIGHEST

WEIGHT = [1.0 - 0.5 * ((t - RADIUS) / RADIUS) ** 2 for t in range(TAPS)]


def ramp(a):
    return (a * (a + 1) * (2 * a + 1)).astype(F32) * (1.0 / 6.0)


def coverage(place, total):
    low = jnp.minimum(place, RADIUS)
    high = jnp.minimum(total - 1 - place, RADIUS)
    return (low + high + 1).astype(F32) - (ramp(low) + ramp(high)) * (0.5 / RADIUS**2)


def band(offset):
    ratio = offset.astype(F32) * (1.0 / RADIUS)
    return jnp.where(jnp.abs(offset) <= RADIUS, 1.0 - 0.5 * ratio * ratio, 0.0)


def lookup(bits, table):
    level = [table[k] for k in range(8)]
    for bit in bits:
        level = [jnp.where(bit, level[k + 1], level[k]) for k in range(0, len(level), 2)]
    return level[0]


def taps(rows):
    total = rows(RADIUS)
    for t in range(RADIUS):
        total = total + WEIGHT[t] * (rows(t) + rows(TAPS - 1 - t))
    return total


def kernel(
    ngx, ngy,
    disp, vel, hist, zone, modulus, threshold, density,
    nd_out, nv_out, nh_out,
    de, v, h, z, fys, fy, er, e, yb, out, xr, u, tm, rm, ix, iy, pxs, px, pys, py, pyi, nd, nv, nh,
    lsem, ssem, rsem,
):
    gx = lax.axis_index("gx")
    gy = lax.axis_index("gy")
    where_am = {"gx": gx, "gy": gy}
    count = {"gx": ngx, "gy": ngy}

    def reach(axis, step):
        place = where_am[axis] + step
        return (place >= 0) & (place < count[axis])

    local = [
        pltpu.make_async_copy(disp, de.at[:, pl.ds(0, N), pl.ds(0, N), :], lsem.at[0]),
        pltpu.make_async_copy(hist, h, lsem.at[1]),
        pltpu.make_async_copy(zone, z, lsem.at[2]),
        pltpu.make_async_copy(vel, v, lsem.at[3]),
    ]
    for copy in local:
        copy.start()

    barrier = pltpu.get_barrier_semaphore()
    partners = jnp.int32(0)
    for axis in ("gx", "gy"):
        for step in (-2, -1, 1, 2):
            ok = reach(axis, step)
            partners = partners + jnp.where(ok, 1, 0)

            @pl.when(ok)
            def _(axis=axis, step=step):
                pl.semaphore_signal(
                    barrier, inc=1, device_id={axis: where_am[axis] + step}, device_id_type=MESH
                )

    made = []

    def remote(src, dst, axis, step):
        k = len(made)
        copy = pltpu.make_async_remote_copy(
            src_ref=src,
            dst_ref=dst,
            send_sem=ssem.at[k],
            recv_sem=rsem.at[k],
            device_id={axis: where_am[axis] + step},
            device_id_type=MESH,
        )
        made.append((copy, axis, step))
        return k

    def start(k):
        copy, axis, step = made[k]
        pl.when(reach(axis, step))(copy.start)

    def arrived(k):
        copy, axis, step = made[k]
        pl.when(reach(axis, -step))(copy.wait_recv)

    def left(k):
        copy, axis, step = made[k]
        pl.when(reach(axis, step))(copy.wait_send)

    def rows(ref, first, number):
        return ref.at[pl.ds(first * N, number * N), :]

    front_x = remote(de.at[:, 0, pl.ds(0, N), :], de.at[:, N, pl.ds(0, N), :], "gx", -1)
    front_y = remote(fys, fy, "gy", -1)
    part_x = []
    for c in range(3):
        span = pl.ds(c * CH, CH)
        src = e.at[pl.ds(25, 23), span, :]
        part_x.append(
            (
                remote(src, e.at[pl.ds(1, 23), span, :], "gx", 1),
                remote(src, e.at[pl.ds(49, 23), span, :], "gx", -1),
            )
        )
    last_x = (
        remote(e.at[48], e.at[24], "gx", 1),
        remote(e.at[48], e.at[72], "gx", -1),
        remote(e.at[48], e.at[0], "gx", 2),
    )
    part_y = []
    for c in range(3):
        src = rows(yb, 25 + c * CH, CH)
        part_y.append(
            (
                remote(src, rows(yb, 1 + c * CH, CH), "gy", 1),
                remote(src, rows(yb, 49 + c * CH, CH), "gy", -1),
            )
        )
    edge_y = (
        remote(rows(yb, 48, 1), rows(yb, 0, 1), "gy", 2),
        remote(xr.at[pl.ds(N, N), :], xr.at[pl.ds(0, N), :], "gy", 1),
        remote(xr.at[pl.ds(N, N), :], xr.at[pl.ds(2 * N, N), :], "gy", -1),
    )
    face_x = remote(pxs, px, "gx", 1)
    face_y = remote(pys, py, "gy", 1)

    zeros = functools.partial(jnp.zeros, dtype=F32)

    @pl.when(gx == 0)
    def _():
        e[pl.ds(0, 25)] = zeros((25, N, DEPTH))
        px[0:3] = zeros((3, N, DEPTH))
        px[3:5] = zeros((2, N, DEPTH)) + 1.0

    @pl.when(gx == 1)
    def _():
        e[0] = zeros((N, DEPTH))

    @pl.when(gx == ngx - 1)
    def _():
        e[pl.ds(49, 24)] = zeros((24, N, DEPTH))
        for j in range(3):
            de[j, N, 0:N, :] = zeros((N, DEPTH))

    @pl.when(gy == 0)
    def _():
        yb[0 : 25 * N] = zeros((25 * N, DEPTH))
        xr[0:N] = zeros((N, DEPTH))
        py[0:3] = zeros((3, N, DEPTH))
        py[3:5] = zeros((2, N, DEPTH)) + 1.0

    @pl.when(gy == 1)
    def _():
        yb[0:N] = zeros((N, DEPTH))

    @pl.when(gy == ngy - 1)
    def _():
        yb[49 * N : 73 * N] = zeros((24 * N, DEPTH))
        xr[2 * N : 3 * N] = zeros((N, DEPTH))
        fy[...] = zeros((3, N, DEPTH))

    left_z = lax.broadcasted_iota(jnp.int32, (DEPTH, DEPTH), 0)
    right_z = lax.broadcasted_iota(jnp.int32, (DEPTH, DEPTH), 1)
    band_z = band(right_z - left_z) / coverage(right_z, DEPTH)
    place = lax.broadcasted_iota(jnp.int32, (25, CH, DEPTH), 0) - 1
    ix[...] = 1.0 / coverage(gx * N + place, ngx * N)
    iy[...] = 1.0 / coverage(gy * N + place, ngy * N)

    def along_z(block):
        shape = block.shape
        flat = block.reshape(-1, DEPTH)
        return jnp.dot(flat, band_z, precision=HIGHEST, preferred_element_type=F32).reshape(shape)

    def gradients(i, y0, y1):
        lane = lax.broadcasted_iota(jnp.int32, (y1 - y0, DEPTH), 1)
        centre = [de[j, i, y0:y1, :] for j in range(3)]
        ahead = [
            [de[j, i + 1, y0:y1, :] for j in range(3)],
            [de[j, i, y0 + 1 : y1 + 1, :] for j in range(3)],
            [jnp.where(lane < DEPTH - 1, pltpu.roll(centre[j], DEPTH - 1, 1), 0.0) for j in range(3)],
        ]
        return [[ahead[a][j] - centre[j] for j in range(3)] for a in range(3)]

    def equivalent(i, y0, y1):
        g = gradients(i, y0, y1)
        xy, xz, yz = g[0][1] + g[1][0], g[0][2] + g[2][0], g[1][2] + g[2][1]
        squares = g[0][0] * g[0][0] + g[1][1] * g[1][1] + g[2][2] * g[2][2]
        squares = squares + 0.5 * (xy * xy + xz * xz + yz * yz)
        er[i, y0:y1, :] = jnp.sqrt(squares)

    local[0].wait()
    for j in range(3):
        fys[j] = de[j, 0:N, 0, :]

    def early(i, carry):
        equivalent(i, 0, 16)
        return carry

    lax.fori_loop(0, N - 1, early, 0)
    e[pl.ds(25, 23), 0:16, :] = along_z(er[pl.ds(0, 23), 0:16, :])

    pl.semaphore_wait(barrier, partners)
    start(front_x)
    start(front_y)
    for c in range(2):
        for k in part_x[c]:
            start(k)

    local[1].wait()
    local[2].wait()

    def material(i, carry):
        zz = z[i]
        bits = [(zz & 1) != 0, (zz & 2) != 0, (zz & 4) != 0]
        tm[i] = lookup(bits, threshold)
        rm[i] = 0.1 / lookup(bits, density)
        u[5, i] = lookup(bits, modulus)
        return carry

    lax.fori_loop(0, N, material, 0)

    arrived(front_x)
    arrived(front_y)
    for j in range(3):
        de[j, 0:N, N, :] = fy[j]

    def late(i, carry):
        equivalent(i, 16, 24)
        return carry

    lax.fori_loop(0, N - 1, late, 0)
    equivalent(N - 1, 0, N)
    e[48] = along_z(er[N - 1])
    for k in last_x:
        start(k)
    e[pl.ds(25, 23), 16:24, :] = along_z(er[pl.ds(0, 23), 16:24, :])
    for k in part_x[2]:
        start(k)

    def undamaged(i, carry):
        g = gradients(i, 0, N)
        mu = u[5, i]
        trace = mu * (g[0][0] + g[1][1] + g[2][2])
        xy, yy, yz = mu * (g[0][1] + g[1][0]), trace + 2.0 * mu * g[1][1], mu * (g[1][2] + g[2][1])
        u[0, i] = trace + 2.0 * mu * g[0][0]
        u[1, i] = xy
        u[2, i] = mu * (g[0][2] + g[2][0])
        u[3, i] = yy
        u[4, i] = yz
        u[5, i] = trace + 2.0 * mu * g[2][2]
        return carry

    lax.fori_loop(0, N, undamaged, 0)
    for k, source in enumerate((u.at[0], u.at[1], u.at[2], h, tm)):
        pxs[k] = source[N - 1]
    for k, source in enumerate((u.at[1], u.at[3], u.at[4], h, tm)):
        pys[k] = source[0:N, N - 1, :]
    start(face_x)
    start(face_y)

    for c in range(3):
        for k in part_x[c]:
            arrived(k)
        if c == 0:
            for k in last_x:
                arrived(k)
        span = slice(c * CH, (c + 1) * CH)
        middle = taps(lambda t: e[t : t + 25, span, :]) * ix[...]
        xr[N + c * CH : N + (c + 1) * CH, :] = middle[0]
        for i in range(N):
            yb[pl.ds((25 + c * CH) * N + i, CH, stride=N), :] = middle[i + 1]
        for k in part_y[c]:
            start(k)
    for k in edge_y:
        start(k)

    for c in range(3):
        for k in part_y[c]:
            arrived(k)
    for k in edge_y:
        arrived(k)

    def across(g, carry):
        off = pl.multiple_of(g * CH, CH)
        read = lambda t: jnp.stack([yb[pl.ds((m + t) * N + off, CH), :] for m in range(25)])
        total = taps(read) * iy[...]
        for m in range(25):
            out[pl.ds(m * N + off, CH), :] = total[m]
        return carry

    lax.fori_loop(0, N // CH, across, 0)

    arrived(face_x)
    arrived(face_y)

    def intact(history, average, limit):
        bounded = jnp.maximum(jnp.maximum(history, average), limit)
        return limit / bounded * jnp.exp(-0.5 * (bounded - limit))

    row = lax.broadcasted_iota(jnp.int32, (N, 3 * N), 0)
    col = lax.broadcasted_iota(jnp.int32, (N, 3 * N), 1)
    weights = band(col - N - row) / coverage(gy * N + row, ngy * N)
    average_x = jnp.dot(weights, xr[...], precision=HIGHEST, preferred_element_type=F32)
    whole_x = intact(px[3], average_x, px[4])
    whole_y = intact(py[3], out[0:N, :], py[4])
    for j in range(3):
        pyi[j] = whole_y * py[j]

    local[3].wait()
    lane = lax.broadcasted_iota(jnp.int32, (N, DEPTH), 1)
    sub = lax.broadcasted_iota(jnp.int32, (N, DEPTH), 0)

    def finish(i, before):
        average = out[pl.ds(N + i, N, stride=N), :]
        top = jnp.maximum(h[i], average)
        nh[i] = top
        limit = tm[i]
        bounded = jnp.maximum(top, limit)
        whole = limit / bounded * jnp.exp(-0.5 * (bounded - limit))
        s = [whole * u[k, i] for k in range(6)]
        sx, sy, sz = (s[0], s[1], s[2]), (s[1], s[3], s[4]), (s[2], s[4], s[5])
        rate = rm[i]
        for j in range(3):
            back_y = jnp.where(sub > 0, pltpu.roll(sy[j], 1, 0), pyi[j, pl.ds(i, 1), :])
            back_z = jnp.where(lane > 0, pltpu.roll(sz[j], 1, 1), 0.0)
            force = sx[j] - before[j] + (sy[j] - back_y) + (sz[j] - back_z)
            speed = v[j, i] + rate * force
            nv[j, i] = speed
            nd[j, i] = de[j, i, 0:N, :] + 0.1 * speed
        return sx

    lax.fori_loop(0, N, finish, tuple(whole_x * px[j] for j in range(3)))

    done = [
        pltpu.make_async_copy(nd, nd_out, lsem.at[0]),
        pltpu.make_async_copy(nv, nv_out, lsem.at[1]),
        pltpu.make_async_copy(nh, nh_out, lsem.at[2]),
    ]
    for copy in done:
        copy.start()
    for k in range(len(made)):
        left(k)
    for copy in done:
        copy.wait()


COPIES = 22


def body(ngx, ngy, displacement, velocity, history, zone, zone_modulus, zone_threshold, zone_density):
    block = (N, N, DEPTH)
    plane = (N, DEPTH)
    anywhere = pl.BlockSpec(memory_space=pl.ANY)
    table = pl.BlockSpec(memory_space=pltpu.SMEM)
    vmem = lambda *shape: pltpu.VMEM(shape, F32)
    return pl.pallas_call(
        functools.partial(kernel, ngx, ngy),
        out_shape=(
            jax.ShapeDtypeStruct((3, *block), F32),
            jax.ShapeDtypeStruct((3, *block), F32),
            jax.ShapeDtypeStruct(block, F32),
        ),
        in_specs=[anywhere] * 4 + [table] * 3,
        out_specs=(anywhere, anywhere, anywhere),
        scratch_shapes=[
            vmem(3, N + 1, 32, DEPTH),
            vmem(3, *block),
            vmem(*block),
            pltpu.VMEM(block, jnp.int32),
            vmem(3, *plane),
            vmem(3, *plane),
            vmem(*block),
            vmem(73, *plane),
            vmem(73 * N, DEPTH),
            vmem(25 * N, DEPTH),
            vmem(3 * N, DEPTH),
            vmem(6, *block),
            vmem(*block),
            vmem(*block),
            vmem(25, CH, DEPTH),
            vmem(25, CH, DEPTH),
            vmem(5, *plane),
            vmem(5, *plane),
            vmem(5, *plane),
            vmem(5, *plane),
            vmem(3, *plane),
            vmem(3, *block),
            vmem(3, *block),
            vmem(*block),
            pltpu.SemaphoreType.DMA((4,)),
            pltpu.SemaphoreType.DMA((COPIES,)),
            pltpu.SemaphoreType.DMA((COPIES,)),
        ],
        compiler_params=pltpu.CompilerParams(
            collective_id=0, has_side_effects=True, vmem_limit_bytes=40 * 1024 * 1024
        ),
    )(displacement, velocity, history, zone, zone_modulus, zone_threshold, zone_density)


def solution(mesh):
    return jax.shard_map(
        functools.partial(body, mesh.shape["gx"], mesh.shape["gy"]),
        mesh=mesh,
        in_specs=(
            P(None, "gx", "gy", None),
            P(None, "gx", "gy", None),
            P("gx", "gy", None),
            P("gx", "gy", None),
            P(),
            P(),
            P(),
        ),
        out_specs=(P(None, "gx", "gy", None), P(None, "gx", "gy", None), P("gx", "gy", None)),
        check_vma=False,
    )
```

time: 97.3 us -> 61.8 us (0.64); the launches traced: 95.6 us -> 61.5 us
  Pallas kernels: 0 us -> 52.1 us
  starting transfers between devices: 36.4 us -> 0 us
  waiting for transfers between devices: 28.9 us -> 0 us
  matrix products: 13.2 us -> 0 us
  other arithmetic: 8.51 us -> 0 us
  local copies, waits for them, and re-layouts: 7.62 us -> 8.75 us
    pallas_call x0 -> x1, Pallas kernels: none -> 52.1 us  [body(): pl.pallas_call(functools.partial(kernel, ngx, ngy), out_shape=(jax.ShapeD...]
    ppermute x8 -> x0, starting transfers between devices: 36.4 us -> none  [the longest x4 15.7 us: passed_along(): return lax.ppermute(shard, axis, pairs)]
    ppermute x8 -> x0, waiting for transfers between devices: 28.9 us -> none  [the longest x2 12.2 us: padded(): lax.ppermute(lax.slice_in_dim(block, 0, width, axis=dim), axis, backward)]
    dot_general x3 -> x0, matrix products: 13.2 us -> none  [the longest x1 11.9 us: pass_cols(): jnp.einsum('ab,xbz->xaz', weights, block, precision=lax.Precision.HIGHEST)]
    unnamed x14 -> x17, local copies, waits for them, and re-layouts: 2.06 us -> 8.75 us
    slice x16 -> x0, local copies, waits for them, and re-layouts: 5.54 us -> none  [the longest x3 2.05 us: lookup(): result = jnp.where(zone == level, table[level], result)]
    select_n x1 -> x0, other arithmetic: 5.51 us -> none  [lookup(): result = jnp.where(zone == level, table[level], result)]
    add x3 -> x0, other arithmetic: 1.4 us -> none  [the longest x1 1.39 us: body(): new_displacement = displacement + time_step * new_velocity]
  transfers between devices with their start and end apart: 8 -> 0, of which waited for: 4 -> 0; matrix products, arithmetic and copies ran while one was open for 11% -> 0% of each run, Pallas kernels for 0% -> 0%
where the time goes in v1:
time: 61.8 us; the launch traced here: 61.5 us
  Pallas kernels  52.1 us (84%)
  local copies, waits for them, and re-layouts  8.75 us (14%)
  between operations  0.66 us (1%)
    pallas_call x1, Pallas kernels, body(): pl.pallas_call(functools.partial(kernel, ngx, ngy), out_shape=(jax.ShapeD...  52.1 us
    unnamed x17, local copies, waits for them, and re-layouts  8.75 us

profile of v1, /device:TPU:7, one launch (start us, length us, event | category | flops | bytes accessed | tf_op | source)
XLA Modules:
  0.0 61.5 jit_solution(1052012837101872731)
XLA Ops:
  0.6 0.0 copy-start
  0.6 1.2 %copy-done = f32[3,24,24,128]{3,2,1,0:T(8,128)S(1)} copy-done((f32[3,24,24,128]{3,2,1,0:T(8,128)S(1)}, f32[3,24,24,128]{3,2,1,0:T(8,128)}, u32[]{:S(2)}) %copy-start) | copy-done | bytes 884760
  1.8 0.0 copy-start.1
  1.8 1.2 %copy-done.1 = f32[3,24,24,128]{3,2,1,0:T(8,128)S(1)} copy-done((f32[3,24,24,128]{3,2,1,0:T(8,128)S(1)}, f32[3,24,24,128]{3,2,1,0:T(8,128)}, u32[]{:S(2)}) %copy-start.1) | copy-done | bytes 884760
  3.0 0.0 copy-start.2
  3.0 1.0 %copy-done.2 = f32[24,24,128]{2,1,0:T(8,128)S(1)} copy-done((f32[24,24,128]{2,1,0:T(8,128)S(1)}, f32[24,24,128]{2,1,0:T(8,128)}, u32[]{:S(2)}) %copy-start.2) | copy-done | bytes 294936
  3.9 0.0 copy-start.3
  3.9 1.0 %copy-done.3 = s32[24,24,128]{2,1,0:T(8,128)S(1)} copy-done((s32[24,24,128]{2,1,0:T(8,128)S(1)}, s32[24,24,128]{2,1,0:T(8,128)}, u32[]{:S(2)}) %copy-start.3) | copy-done | bytes 294936
  4.9 0.0 copy-start.4
  4.9 0.7 %copy-done.4 = f32[8]{0:T(128)S(1)} copy-done((f32[8]{0:T(128)S(1)}, f32[8]{0:T(128)}, u32[]{:S(2)}) %copy-start.4) | copy-done | bytes 56
  5.5 0.0 copy-start.5
  5.6 0.7 %copy-done.5 = f32[8]{0:T(128)S(1)} copy-done((f32[8]{0:T(128)S(1)}, f32[8]{0:T(128)}, u32[]{:S(2)}) %copy-start.5) | copy-done | bytes 56
  6.2 0.0 copy-start.6
  6.2 0.7 %copy-done.6 = f32[8]{0:T(128)S(1)} copy-done((f32[8]{0:T(128)S(1)}, f32[8]{0:T(128)}, u32[]{:S(2)}) %copy-start.6) | copy-done | bytes 56
  6.9 52.1 %shard_map.94 = (f32[3,24,24,128]{3,2,1,0:T(8,128)S(1)}, f32[3,24,24,128]{3,2,1,0:T(8,128)S(1)}, f32[24,24,128]{2,1,0:T(8,128)S(1)}) custom-call(f32[3,24,24,128]{3,2,1,0:T(8,128)S(1)} %copy-done, f32[3,24,24,128]{3,2,1,0:T(8,128)S(1)} %copy-done.1, f32[24,24,128]{2,1,0:T(8,128)S(1)} %copy-done.2, s32[24,24,128]{2,1,0:T(8,128)S(1)} %copy-done.3, ...), custom_call_target="tpu_custom_call" | custom-call | tf_op jit(solution)/shard_map/pallas_call | solution.py:382
  59.0 0.9 %copy.13 = f32[3,24,24,128]{3,2,1,0:T(8,128)} copy(f32[3,24,24,128]{3,2,1,0:T(8,128)S(1)} %get-tuple-element.6) | data formatting | bytes 1769472
  59.9 0.9 %copy.14 = f32[3,24,24,128]{3,2,1,0:T(8,128)} copy(f32[3,24,24,128]{3,2,1,0:T(8,128)S(1)} %get-tuple-element.7) | data formatting | bytes 1769472
  60.8 0.7 %copy.15 = f32[24,24,128]{2,1,0:T(8,128)} copy(f32[24,24,128]{2,1,0:T(8,128)S(1)} %get-tuple-element.8) | data formatting | bytes 589824
Async XLA Ops:
  0.6 1.2 %copy-start = (f32[3,24,24,128]{3,2,1,0:T(8,128)S(1)}, f32[3,24,24,128]{3,2,1,0:T(8,128)}, u32[]{:S(2)}) copy-start(f32[3,24,24,128]{3,2,1,0:T(8,128)} %disp.1) | copy-start | bytes 2654212
  1.8 1.2 %copy-start.1 = (f32[3,24,24,128]{3,2,1,0:T(8,128)S(1)}, f32[3,24,24,128]{3,2,1,0:T(8,128)}, u32[]{:S(2)}) copy-start(f32[3,24,24,128]{3,2,1,0:T(8,128)} %vel.1) | copy-start | bytes 2654212
  3.0 1.0 %copy-start.2 = (f32[24,24,128]{2,1,0:T(8,128)S(1)}, f32[24,24,128]{2,1,0:T(8,128)}, u32[]{:S(2)}) copy-start(f32[24,24,128]{2,1,0:T(8,128)} %hist.1) | copy-start | bytes 884740
  3.9 1.0 %copy-start.3 = (s32[24,24,128]{2,1,0:T(8,128)S(1)}, s32[24,24,128]{2,1,0:T(8,128)}, u32[]{:S(2)}) copy-start(s32[24,24,128]{2,1,0:T(8,128)} %zone.1) | copy-start | bytes 884740
  4.9 0.7 %copy-start.4 = (f32[8]{0:T(128)S(1)}, f32[8]{0:T(128)}, u32[]{:S(2)}) copy-start(f32[8]{0:T(128)} %modulus.1) | copy-start | bytes 100
  5.5 0.7 %copy-start.5 = (f32[8]{0:T(128)S(1)}, f32[8]{0:T(128)}, u32[]{:S(2)}) copy-start(f32[8]{0:T(128)} %threshold.1) | copy-start | bytes 100
  6.2 0.7 %copy-start.6 = (f32[8]{0:T(128)S(1)}, f32[8]{0:T(128)}, u32[]{:S(2)}) copy-start(f32[8]{0:T(128)} %density.1) | copy-start | bytes 100

commit v2 on v1

--- a/solution.py
+++ b/solution.py
@@ -50,10 +50,10 @@
 
 def kernel(
     ngx, ngy,
-    disp, vel, hist, zone, modulus, threshold, density,
-    nd_out, nv_out, nh_out,
-    de, v, h, z, fys, fy, er, e, yb, out, xr, u, tm, rm, ix, iy, pxs, px, pys, py, pyi, nd, nv, nh,
-    lsem, ssem, rsem,
+    disp, vel, hist, zone, modulus_in, threshold_in, density_in,
+    nd, nv, nh,
+    de, v, h, z, fys, fy, er, e, yb, out, xr, u, tm, rm, ix, iy, pxs, px, pys, py, pyi,
+    modulus, threshold, density, lsem, ssem, rsem,
 ):
     gx = lax.axis_index("gx")
     gy = lax.axis_index("gy")
@@ -69,6 +69,9 @@
         pltpu.make_async_copy(hist, h, lsem.at[1]),
         pltpu.make_async_copy(zone, z, lsem.at[2]),
         pltpu.make_async_copy(vel, v, lsem.at[3]),
+        pltpu.make_async_copy(modulus_in, modulus, lsem.at[4]),
+        pltpu.make_async_copy(threshold_in, threshold, lsem.at[5]),
+        pltpu.make_async_copy(density_in, density, lsem.at[6]),
     ]
     for copy in local:
         copy.start()
@@ -222,7 +225,7 @@
         equivalent(i, 0, 16)
         return carry
 
-    lax.fori_loop(0, N - 1, early, 0)
+    lax.fori_loop(0, N - 1, early, 0, unroll=True)
     e[pl.ds(25, 23), 0:16, :] = along_z(er[pl.ds(0, 23), 0:16, :])
 
     pl.semaphore_wait(barrier, partners)
@@ -232,8 +235,8 @@
         for k in part_x[c]:
             start(k)
 
-    local[1].wait()
-    local[2].wait()
+    for k in (1, 2, 4, 5, 6):
+        local[k].wait()
 
     def material(i, carry):
         zz = z[i]
@@ -243,7 +246,7 @@
         u[5, i] = lookup(bits, modulus)
         return carry
 
-    lax.fori_loop(0, N, material, 0)
+    lax.fori_loop(0, N, material, 0, unroll=4)
 
     arrived(front_x)
     arrived(front_y)
@@ -254,7 +257,7 @@
         equivalent(i, 16, 24)
         return carry
 
-    lax.fori_loop(0, N - 1, late, 0)
+    lax.fori_loop(0, N - 1, late, 0, unroll=True)
     equivalent(N - 1, 0, N)
     e[48] = along_z(er[N - 1])
     for k in last_x:
@@ -276,7 +279,7 @@
         u[5, i] = trace + 2.0 * mu * g[2][2]
         return carry
 
-    lax.fori_loop(0, N, undamaged, 0)
+    lax.fori_loop(0, N, undamaged, 0, unroll=4)
     for k, source in enumerate((u.at[0], u.at[1], u.at[2], h, tm)):
         pxs[k] = source[N - 1]
     for k, source in enumerate((u.at[1], u.at[3], u.at[4], h, tm)):
@@ -355,17 +358,19 @@
             nd[j, i] = de[j, i, 0:N, :] + 0.1 * speed
         return sx
 
-    lax.fori_loop(0, N, finish, tuple(whole_x * px[j] for j in range(3)))
-
+    lax.fori_loop(0, N, finish, tuple(whole_x * px[j] for j in range(3)), unroll=4)
+
+    for k in range(len(made)):
+        left(k)
+
+
+def store(nd, nv, nh, nd_out, nv_out, nh_out, sem):
     done = [
-        pltpu.make_async_copy(nd, nd_out, lsem.at[0]),
-        pltpu.make_async_copy(nv, nv_out, lsem.at[1]),
-        pltpu.make_async_copy(nh, nh_out, lsem.at[2]),
+        pltpu.make_async_copy(source, target, sem.at[k])
+        for k, (source, target) in enumerate(((nd, nd_out), (nv, nv_out), (nh, nh_out)))
     ]
     for copy in done:
         copy.start()
-    for k in range(len(made)):
-        left(k)
     for copy in done:
         copy.wait()
 
@@ -376,18 +381,15 @@
 def body(ngx, ngy, displacement, velocity, history, zone, zone_modulus, zone_threshold, zone_density):
     block = (N, N, DEPTH)
     plane = (N, DEPTH)
-    anywhere = pl.BlockSpec(memory_space=pl.ANY)
-    table = pl.BlockSpec(memory_space=pltpu.SMEM)
+    whole = pl.BlockSpec(memory_space=pltpu.VMEM)
+    fixed = pl.BlockSpec(memory_space=pltpu.HBM)
     vmem = lambda *shape: pltpu.VMEM(shape, F32)
-    return pl.pallas_call(
+    hold = lambda array: pltpu.with_memory_space_constraint(array, pltpu.HBM)
+    results = pl.pallas_call(
         functools.partial(kernel, ngx, ngy),
-        out_shape=(
-            jax.ShapeDtypeStruct((3, *block), F32),
-            jax.ShapeDtypeStruct((3, *block), F32),
-            jax.ShapeDtypeStruct(block, F32),
-        ),
-        in_specs=[anywhere] * 4 + [table] * 3,
-        out_specs=(anywhere, anywhere, anywhere),
+        out_shape=(vmem(3, *block), vmem(3, *block), vmem(*block)),
+        in_specs=[fixed] * 7,
+        out_specs=(whole, whole, whole),
         scratch_shapes=[
             vmem(3, N + 1, 32, DEPTH),
             vmem(3, *block),
@@ -410,17 +412,24 @@
             vmem(5, *plane),
             vmem(5, *plane),
             vmem(3, *plane),
-            vmem(3, *block),
-            vmem(3, *block),
-            vmem(*block),
-            pltpu.SemaphoreType.DMA((4,)),
+            pltpu.SMEM((8,), F32),
+            pltpu.SMEM((8,), F32),
+            pltpu.SMEM((8,), F32),
+            pltpu.SemaphoreType.DMA((7,)),
             pltpu.SemaphoreType.DMA((COPIES,)),
             pltpu.SemaphoreType.DMA((COPIES,)),
         ],
         compiler_params=pltpu.CompilerParams(
             collective_id=0, has_side_effects=True, vmem_limit_bytes=40 * 1024 * 1024
         ),
-    )(displacement, velocity, history, zone, zone_modulus, zone_threshold, zone_density)
+    )(*(hold(a) for a in (displacement, velocity, history, zone, zone_modulus, zone_threshold, zone_density)))
+    return pl.pallas_call(
+        store,
+        out_shape=tuple(jax.ShapeDtypeStruct(r.shape, F32) for r in results),
+        in_specs=[whole] * 3,
+        out_specs=(fixed,) * 3,
+        scratch_shapes=[pltpu.SemaphoreType.DMA((3,))],
+    )(*(pltpu.with_memory_space_constraint(r, pltpu.VMEM) for r in results))
 
 
 def solution(mesh):

time: 61.8 us -> 51.4 us (0.83)
  local copies, waits for them, and re-layouts: 8.75 us -> 0 us
  Pallas kernels: 52.1 us -> 50.6 us
    unnamed x17 -> x0, local copies, waits for them, and re-layouts: 8.75 us -> none
    pallas_call x1 -> x2, Pallas kernels: 52.1 us -> 50.6 us  [the longest x1 49.3 us: body(): pl.pallas_call(functools.partial(kernel, ngx, ngy), out_shape=(vmem(3, *b...]
where the time goes in v2:
time: 51.4 us; the launch traced here: 51.2 us
  Pallas kernels  50.6 us (98%)
  between operations  0.64 us (1%)
    pallas_call x1, Pallas kernels, body(): pl.pallas_call(functools.partial(kernel, ngx, ngy), out_shape=(vmem(3, *b...  49.3 us
    pallas_call x1, Pallas kernels, body(): pl.pallas_call(store, out_shape=tuple((jax.ShapeDtypeStruct(r.shape, F32)...  1.32 us

profile of v2, /device:TPU:7, one launch (start us, length us, event | category | flops | bytes accessed | tf_op | source)
XLA Modules:
  0.0 51.2 jit_solution(18330315044548542321)
XLA Ops:
  0.6 49.3 %shard_map.94 = (f32[3,24,24,128]{3,2,1,0:T(8,128)S(1)}, f32[3,24,24,128]{3,2,1,0:T(8,128)S(1)}, f32[24,24,128]{2,1,0:T(8,128)S(1)}) custom-call(f32[3,24,24,128]{3,2,1,0:T(8,128)} %disp.1, f32[3,24,24,128]{3,2,1,0:T(8,128)} %vel.1, f32[24,24,128]{2,1,0:T(8,128)} %hist.1, s32[24,24,128]{2,1,0:T(8,128)} %zone.1, f32[8]{0:T(128)} %modulus_in.1, ...), custom_call_target="tpu_custom_call" | custom-call | tf_op jit(solution)/shard_map/pallas_call | solution.py:388
  49.9 1.3 %shard_map.95 = (f32[3,24,24,128]{3,2,1,0:T(8,128)}, f32[3,24,24,128]{3,2,1,0:T(8,128)}, f32[24,24,128]{2,1,0:T(8,128)}) custom-call(f32[3,24,24,128]{3,2,1,0:T(8,128)S(1)} %get-tuple-element.6.nd, f32[3,24,24,128]{3,2,1,0:T(8,128)S(1)} %get-tuple-element.7.nv, f32[24,24,128]{2,1,0:T(8,128)S(1)} %get-tuple-element.8.nh), custom_call_target="tpu_custom_call" | custom-call | tf_op jit(solution)/shard_map/pallas_call | solution.py:426

commit v3 on v2

--- a/solution.py
+++ b/solution.py
@@ -52,7 +52,7 @@
     ngx, ngy,
     disp, vel, hist, zone, modulus_in, threshold_in, density_in,
     nd, nv, nh,
-    de, v, h, z, fys, fy, er, e, yb, out, xr, u, tm, rm, ix, iy, pxs, px, pys, py, pyi,
+    de, v, h, z, fys, fy, er, e, yb, out, xr, u, tm, rm, ix, iy, ie, pxs, px, pys, py, pyi,
     modulus, threshold, density, lsem, ssem, rsem,
 ):
     gx = lax.axis_index("gx")
@@ -79,7 +79,7 @@
     barrier = pltpu.get_barrier_semaphore()
     partners = jnp.int32(0)
     for axis in ("gx", "gy"):
-        for step in (-2, -1, 1, 2):
+        for step in (-1, 1):
             ok = reach(axis, step)
             partners = partners + jnp.where(ok, 1, 0)
 
@@ -108,6 +108,17 @@
         copy, axis, step = made[k]
         pl.when(reach(axis, step))(copy.start)
 
+    def far(step):
+        return lax.rem(gx, 4) == (3 if step > 0 else 0)
+
+    def start_far(k):
+        copy, axis, step = made[k]
+        pl.when(reach(axis, step) & far(step))(copy.start)
+
+    def start_near(k):
+        copy, axis, step = made[k]
+        pl.when(reach(axis, step) & jnp.logical_not(far(step)))(copy.start)
+
     def arrived(k):
         copy, axis, step = made[k]
         pl.when(reach(axis, -step))(copy.wait_recv)
@@ -123,18 +134,17 @@
     front_y = remote(fys, fy, "gy", -1)
     part_x = []
     for c in range(3):
-        span = pl.ds(c * CH, CH)
-        src = e.at[pl.ds(25, 23), span, :]
+        src = e.at[c, pl.ds(25, 23)]
         part_x.append(
             (
-                remote(src, e.at[pl.ds(1, 23), span, :], "gx", 1),
-                remote(src, e.at[pl.ds(49, 23), span, :], "gx", -1),
+                remote(src, e.at[c, pl.ds(1, 23)], "gx", 1),
+                remote(src, e.at[c, pl.ds(49, 23)], "gx", -1),
             )
         )
     last_x = (
-        remote(e.at[48], e.at[24], "gx", 1),
-        remote(e.at[48], e.at[72], "gx", -1),
-        remote(e.at[48], e.at[0], "gx", 2),
+        remote(e.at[:, 48], e.at[:, 24], "gx", 1),
+        remote(e.at[:, 48], e.at[:, 72], "gx", -1),
+        remote(e.at[:, 48], e.at[:, 0], "gx", 2),
     )
     part_y = []
     for c in range(3):
@@ -157,17 +167,17 @@
 
     @pl.when(gx == 0)
     def _():
-        e[pl.ds(0, 25)] = zeros((25, N, DEPTH))
+        e[:, 0:25] = zeros((3, 25, CH, DEPTH))
         px[0:3] = zeros((3, N, DEPTH))
         px[3:5] = zeros((2, N, DEPTH)) + 1.0
 
     @pl.when(gx == 1)
     def _():
-        e[0] = zeros((N, DEPTH))
+        e[:, 0] = zeros((3, CH, DEPTH))
 
     @pl.when(gx == ngx - 1)
     def _():
-        e[pl.ds(49, 24)] = zeros((24, N, DEPTH))
+        e[:, 49:73] = zeros((3, 24, CH, DEPTH))
         for j in range(3):
             de[j, N, 0:N, :] = zeros((N, DEPTH))
 
@@ -193,7 +203,10 @@
     band_z = band(right_z - left_z) / coverage(right_z, DEPTH)
     place = lax.broadcasted_iota(jnp.int32, (25, CH, DEPTH), 0) - 1
     ix[...] = 1.0 / coverage(gx * N + place, ngx * N)
+    place = lax.broadcasted_iota(jnp.int32, (N, DEPTH), 0)
     iy[...] = 1.0 / coverage(gy * N + place, ngy * N)
+    edge = lax.broadcasted_iota(jnp.int32, (CH, DEPTH), 0) - 1
+    ie[...] = 1.0 / coverage(gy * N + edge, ngy * N)
 
     def along_z(block):
         shape = block.shape
@@ -215,7 +228,9 @@
         xy, xz, yz = g[0][1] + g[1][0], g[0][2] + g[2][0], g[1][2] + g[2][1]
         squares = g[0][0] * g[0][0] + g[1][1] * g[1][1] + g[2][2] * g[2][2]
         squares = squares + 0.5 * (xy * xy + xz * xz + yz * yz)
-        er[i, y0:y1, :] = jnp.sqrt(squares)
+        root = jnp.sqrt(squares)
+        for c in range(y0 // CH, y1 // CH):
+            er[c, i] = root[c * CH - y0 : (c + 1) * CH - y0]
 
     local[0].wait()
     for j in range(3):
@@ -226,14 +241,14 @@
         return carry
 
     lax.fori_loop(0, N - 1, early, 0, unroll=True)
-    e[pl.ds(25, 23), 0:16, :] = along_z(er[pl.ds(0, 23), 0:16, :])
+    e[0:2, 25:48] = along_z(er[0:2, 0:23])
 
     pl.semaphore_wait(barrier, partners)
     start(front_x)
     start(front_y)
     for c in range(2):
         for k in part_x[c]:
-            start(k)
+            start_far(k)
 
     for k in (1, 2, 4, 5, 6):
         local[k].wait()
@@ -249,6 +264,8 @@
     lax.fori_loop(0, N, material, 0, unroll=4)
 
     arrived(front_x)
+    for k in part_x[0]:
+        start_near(k)
     arrived(front_y)
     for j in range(3):
         de[j, 0:N, N, :] = fy[j]
@@ -259,12 +276,15 @@
 
     lax.fori_loop(0, N - 1, late, 0, unroll=True)
     equivalent(N - 1, 0, N)
-    e[48] = along_z(er[N - 1])
+    e[:, 48] = along_z(er[:, N - 1])
     for k in last_x:
         start(k)
-    e[pl.ds(25, 23), 16:24, :] = along_z(er[pl.ds(0, 23), 16:24, :])
+    e[2, 25:48] = along_z(er[2, 0:23])
     for k in part_x[2]:
-        start(k)
+        start_far(k)
+    for c in (1, 2):
+        for k in part_x[c]:
+            start_near(k)
 
     def undamaged(i, carry):
         g = gradients(i, 0, N)
@@ -293,8 +313,7 @@
         if c == 0:
             for k in last_x:
                 arrived(k)
-        span = slice(c * CH, (c + 1) * CH)
-        middle = taps(lambda t: e[t : t + 25, span, :]) * ix[...]
+        middle = taps(lambda t: e[c, t : t + 25]) * ix[...]
         xr[N + c * CH : N + (c + 1) * CH, :] = middle[0]
         for i in range(N):
             yb[pl.ds((25 + c * CH) * N + i, CH, stride=N), :] = middle[i + 1]
@@ -303,21 +322,35 @@
     for k in edge_y:
         start(k)
 
+    def gather(first, number, fresh):
+        def group(g, carry):
+            off = pl.multiple_of(g * CH, CH)
+            source = jnp.stack([yb[pl.ds((first + k) * N + off, CH), :] for k in range(number)])
+            if fresh:
+                total = jnp.zeros((25, CH, DEPTH), F32)
+            else:
+                total = jnp.stack([out[pl.ds(m * N + off, CH), :] for m in range(25)])
+            for t in range(TAPS):
+                lo, hi = max(0, first - t), min(25, first + number - t)
+                if lo < hi:
+                    part = total[lo:hi] + WEIGHT[t] * source[lo + t - first : hi + t - first]
+                    pieces = [total[:lo]] * (lo > 0) + [part] + [total[hi:]] * (hi < 25)
+                    total = jnp.concatenate(pieces) if len(pieces) > 1 else part
+            for m in range(25):
+                out[pl.ds(m * N + off, CH), :] = total[m]
+            return carry
+
+        lax.fori_loop(0, N // CH, group, 0)
+
+    gather(25, N, True)
     for c in range(3):
         for k in part_y[c]:
             arrived(k)
+        gather(1 + c * CH, CH, False)
+        gather(49 + c * CH, CH, False)
     for k in edge_y:
         arrived(k)
-
-    def across(g, carry):
-        off = pl.multiple_of(g * CH, CH)
-        read = lambda t: jnp.stack([yb[pl.ds((m + t) * N + off, CH), :] for m in range(25)])
-        total = taps(read) * iy[...]
-        for m in range(25):
-            out[pl.ds(m * N + off, CH), :] = total[m]
-        return carry
-
-    lax.fori_loop(0, N // CH, across, 0)
+    out[0:N] += WEIGHT[0] * yb[0:N]
 
     arrived(face_x)
     arrived(face_y)
@@ -331,7 +364,7 @@
     weights = band(col - N - row) / coverage(gy * N + row, ngy * N)
     average_x = jnp.dot(weights, xr[...], precision=HIGHEST, preferred_element_type=F32)
     whole_x = intact(px[3], average_x, px[4])
-    whole_y = intact(py[3], out[0:N, :], py[4])
+    whole_y = intact(py[3], out[0:N, :] * ie[0:1, :], py[4])
     for j in range(3):
         pyi[j] = whole_y * py[j]
 
@@ -340,7 +373,7 @@
     sub = lax.broadcasted_iota(jnp.int32, (N, DEPTH), 0)
 
     def finish(i, before):
-        average = out[pl.ds(N + i, N, stride=N), :]
+        average = out[pl.ds(N + i, N, stride=N), :] * iy[...]
         top = jnp.maximum(h[i], average)
         nh[i] = top
         limit = tm[i]
@@ -397,8 +430,8 @@
             pltpu.VMEM(block, jnp.int32),
             vmem(3, *plane),
             vmem(3, *plane),
-            vmem(*block),
-            vmem(73, *plane),
+            vmem(3, N, CH, DEPTH),
+            vmem(3, 73, CH, DEPTH),
             vmem(73 * N, DEPTH),
             vmem(25 * N, DEPTH),
             vmem(3 * N, DEPTH),
@@ -406,7 +439,8 @@
             vmem(*block),
             vmem(*block),
             vmem(25, CH, DEPTH),
-            vmem(25, CH, DEPTH),
+            vmem(*plane),
+            vmem(CH, DEPTH),
             vmem(5, *plane),
             vmem(5, *plane),
             vmem(5, *plane),

time: 51.4 us -> 46.6 us (0.907)
  the two profiles are of different devices: /device:TPU:7 before, /device:TPU:59 now
where the time goes in v3:
time: 46.6 us; the launch traced here: 46.5 us
  Pallas kernels  45.9 us (98%)
  between operations  0.64 us (1%)
    pallas_call x1, Pallas kernels, body(): pl.pallas_call(functools.partial(kernel, ngx, ngy), out_shape=(vmem(3, *b...  44.5 us
    pallas_call x1, Pallas kernels, body(): pl.pallas_call(store, out_shape=tuple((jax.ShapeDtypeStruct(r.shape, F32)...  1.32 us

profile of v3, /device:TPU:59, one launch (start us, length us, event | category | flops | bytes accessed | tf_op | source)
XLA Modules:
  0.0 46.5 jit_solution(3777948387866341275)
XLA Ops:
  0.6 44.5 %shard_map.94 = (f32[3,24,24,128]{3,2,1,0:T(8,128)S(1)}, f32[3,24,24,128]{3,2,1,0:T(8,128)S(1)}, f32[24,24,128]{2,1,0:T(8,128)S(1)}) custom-call(f32[3,24,24,128]{3,2,1,0:T(8,128)} %disp.1, f32[3,24,24,128]{3,2,1,0:T(8,128)} %vel.1, f32[24,24,128]{2,1,0:T(8,128)} %hist.1, s32[24,24,128]{2,1,0:T(8,128)} %zone.1, f32[8]{0:T(128)} %modulus_in.1, ...), custom_call_target="tpu_custom_call" | custom-call | tf_op jit(solution)/shard_map/pallas_call | solution.py:421
  45.2 1.3 %shard_map.95 = (f32[3,24,24,128]{3,2,1,0:T(8,128)}, f32[3,24,24,128]{3,2,1,0:T(8,128)}, f32[24,24,128]{2,1,0:T(8,128)}) custom-call(f32[3,24,24,128]{3,2,1,0:T(8,128)S(1)} %get-tuple-element.6.nd, f32[3,24,24,128]{3,2,1,0:T(8,128)S(1)} %get-tuple-element.7.nv, f32[24,24,128]{2,1,0:T(8,128)S(1)} %get-tuple-element.8.nh), custom_call_target="tpu_custom_call" | custom-call | tf_op jit(solution)/shard_map/pallas_call | solution.py:460

commit v4 on v3

--- a/solution.py
+++ b/solution.py
@@ -51,8 +51,8 @@
 def kernel(
     ngx, ngy,
     disp, vel, hist, zone, modulus_in, threshold_in, density_in,
-    nd, nv, nh,
-    de, v, h, z, fys, fy, er, e, yb, out, xr, u, tm, rm, ix, iy, ie, pxs, px, pys, py, pyi,
+    de, v, h, u, tm, rm, out, iy, sx0, pyi,
+    z, fys, fx, fy, er, e, yb, xr, ix, ie, pxs, px, pys, py,
     modulus, threshold, density, lsem, ssem, rsem,
 ):
     gx = lax.axis_index("gx")
@@ -130,7 +130,7 @@
     def rows(ref, first, number):
         return ref.at[pl.ds(first * N, number * N), :]
 
-    front_x = remote(de.at[:, 0, pl.ds(0, N), :], de.at[:, N, pl.ds(0, N), :], "gx", -1)
+    front_x = remote(de.at[:, 0, pl.ds(0, N), :], fx, "gx", -1)
     front_y = remote(fys, fy, "gy", -1)
     part_x = []
     for c in range(3):
@@ -169,7 +169,7 @@
     def _():
         e[:, 0:25] = zeros((3, 25, CH, DEPTH))
         px[0:3] = zeros((3, N, DEPTH))
-        px[3:5] = zeros((2, N, DEPTH)) + 1.0
+        px[3] = zeros((N, DEPTH)) + 1.0
 
     @pl.when(gx == 1)
     def _():
@@ -178,15 +178,14 @@
     @pl.when(gx == ngx - 1)
     def _():
         e[:, 49:73] = zeros((3, 24, CH, DEPTH))
-        for j in range(3):
-            de[j, N, 0:N, :] = zeros((N, DEPTH))
+        fx[...] = zeros((3, N, DEPTH))
 
     @pl.when(gy == 0)
     def _():
         yb[0 : 25 * N] = zeros((25 * N, DEPTH))
         xr[0:N] = zeros((N, DEPTH))
         py[0:3] = zeros((3, N, DEPTH))
-        py[3:5] = zeros((2, N, DEPTH)) + 1.0
+        py[3] = zeros((N, DEPTH)) + 1.0
 
     @pl.when(gy == 1)
     def _():
@@ -263,28 +262,39 @@
 
     lax.fori_loop(0, N, material, 0, unroll=4)
 
+    @pl.when(lax.rem(gy, 2) == 0)
+    def _():
+        for k in part_x[0]:
+            start_near(k)
+
     arrived(front_x)
-    for k in part_x[0]:
-        start_near(k)
+
+    @pl.when(lax.rem(gy, 2) == 1)
+    def _():
+        for k in part_x[0]:
+            start_near(k)
+
     arrived(front_y)
     for j in range(3):
+        de[j, N, 0:N, :] = fx[j]
         de[j, 0:N, N, :] = fy[j]
 
     def late(i, carry):
         equivalent(i, 16, 24)
         return carry
 
-    lax.fori_loop(0, N - 1, late, 0, unroll=True)
     equivalent(N - 1, 0, N)
     e[:, 48] = along_z(er[:, N - 1])
     for k in last_x:
         start(k)
+    lax.fori_loop(0, N - 1, late, 0, unroll=True)
     e[2, 25:48] = along_z(er[2, 0:23])
     for k in part_x[2]:
         start_far(k)
-    for c in (1, 2):
-        for k in part_x[c]:
-            start_near(k)
+    for k in part_x[1]:
+        start_near(k)
+    for k in part_x[2]:
+        start_near(k)
 
     def undamaged(i, carry):
         g = gradients(i, 0, N)
@@ -300,27 +310,44 @@
         return carry
 
     lax.fori_loop(0, N, undamaged, 0, unroll=4)
-    for k, source in enumerate((u.at[0], u.at[1], u.at[2], h, tm)):
-        pxs[k] = source[N - 1]
-    for k, source in enumerate((u.at[1], u.at[3], u.at[4], h, tm)):
-        pys[k] = source[0:N, N - 1, :]
-    start(face_x)
-    start(face_y)
+    limit = tm[N - 1]
+    scale = limit * jnp.exp(0.5 * limit)
+    for k in range(3):
+        pxs[k] = scale * u[k, N - 1]
+    pxs[3] = jnp.maximum(h[N - 1], limit)
+    limit = tm[0:N, N - 1, :]
+    scale = limit * jnp.exp(0.5 * limit)
+    for k, source in enumerate((1, 3, 4)):
+        pys[k] = scale * u[source, 0:N, N - 1, :]
+    pys[3] = jnp.maximum(h[0:N, N - 1, :], limit)
+
+    nothing = zeros((1, CH, DEPTH))
+
+    def middle_rows(c, t):
+        if t == 0:
+            return jnp.concatenate([nothing, e[c, 1:25]])
+        return e[c, t : t + 25]
 
     for c in range(3):
         for k in part_x[c]:
             arrived(k)
         if c == 0:
-            for k in last_x:
-                arrived(k)
-        middle = taps(lambda t: e[c, t : t + 25]) * ix[...]
+            arrived(last_x[0])
+            arrived(last_x[1])
+        middle = taps(functools.partial(middle_rows, c)) * ix[...]
         xr[N + c * CH : N + (c + 1) * CH, :] = middle[0]
         for i in range(N):
             yb[pl.ds((25 + c * CH) * N + i, CH, stride=N), :] = middle[i + 1]
         for k in part_y[c]:
             start(k)
-    for k in edge_y:
-        start(k)
+    start(face_x)
+    start(face_y)
+    start(edge_y[0])
+    arrived(last_x[2])
+    for c in range(3):
+        xr[N + c * CH : N + (c + 1) * CH, :] += WEIGHT[0] * ix[0] * e[c, 0]
+    start(edge_y[1])
+    start(edge_y[2])
 
     def gather(first, number, fresh):
         def group(g, carry):
@@ -355,24 +382,32 @@
     arrived(face_x)
     arrived(face_y)
 
-    def intact(history, average, limit):
-        bounded = jnp.maximum(jnp.maximum(history, average), limit)
-        return limit / bounded * jnp.exp(-0.5 * (bounded - limit))
+    def intact(least, average):
+        bounded = jnp.maximum(least, average)
+        return jnp.exp(-0.5 * bounded) / bounded
 
     row = lax.broadcasted_iota(jnp.int32, (N, 3 * N), 0)
     col = lax.broadcasted_iota(jnp.int32, (N, 3 * N), 1)
     weights = band(col - N - row) / coverage(gy * N + row, ngy * N)
     average_x = jnp.dot(weights, xr[...], precision=HIGHEST, preferred_element_type=F32)
-    whole_x = intact(px[3], average_x, px[4])
-    whole_y = intact(py[3], out[0:N, :] * ie[0:1, :], py[4])
+    whole_x = intact(px[3], average_x)
+    whole_y = intact(py[3], out[0:N, :] * ie[0:1, :])
     for j in range(3):
         pyi[j] = whole_y * py[j]
-
+        sx0[j] = whole_x * px[j]
     local[3].wait()
+    for k in range(len(made)):
+        left(k)
+
+
+PARTS = 4
+
+
+def finish(de, v, h, u, tm, rm, out, iy, sx0, pyi, nd_out, nv_out, nh_out, nd, nv, nh, sem):
     lane = lax.broadcasted_iota(jnp.int32, (N, DEPTH), 1)
     sub = lax.broadcasted_iota(jnp.int32, (N, DEPTH), 0)
 
-    def finish(i, before):
+    def row(i, before):
         average = out[pl.ds(N + i, N, stride=N), :] * iy[...]
         top = jnp.maximum(h[i], average)
         nh[i] = top
@@ -391,20 +426,18 @@
             nd[j, i] = de[j, i, 0:N, :] + 0.1 * speed
         return sx
 
-    lax.fori_loop(0, N, finish, tuple(whole_x * px[j] for j in range(3)), unroll=4)
-
-    for k in range(len(made)):
-        left(k)
-
-
-def store(nd, nv, nh, nd_out, nv_out, nh_out, sem):
-    done = [
-        pltpu.make_async_copy(source, target, sem.at[k])
-        for k, (source, target) in enumerate(((nd, nd_out), (nv, nv_out), (nh, nh_out)))
-    ]
-    for copy in done:
-        copy.start()
-    for copy in done:
+    copies = []
+    carry = tuple(sx0[j] for j in range(3))
+    size = N // PARTS
+    for part in range(PARTS):
+        carry = lax.fori_loop(part * size, (part + 1) * size, row, carry, unroll=size)
+        span = pl.ds(part * size, size)
+        for k, (source, target) in enumerate(
+            ((nd.at[:, span], nd_out.at[:, span]), (nv.at[:, span], nv_out.at[:, span]), (nh.at[span], nh_out.at[span]))
+        ):
+            copies.append(pltpu.make_async_copy(source, target, sem.at[3 * part + k]))
+            copies[-1].start()
+    for copy in copies:
         copy.wait()
 
 
@@ -420,32 +453,35 @@
     hold = lambda array: pltpu.with_memory_space_constraint(array, pltpu.HBM)
     results = pl.pallas_call(
         functools.partial(kernel, ngx, ngy),
-        out_shape=(vmem(3, *block), vmem(3, *block), vmem(*block)),
-        in_specs=[fixed] * 7,
-        out_specs=(whole, whole, whole),
-        scratch_shapes=[
+        out_shape=(
             vmem(3, N + 1, 32, DEPTH),
             vmem(3, *block),
             vmem(*block),
+            vmem(6, *block),
+            vmem(*block),
+            vmem(*block),
+            vmem(25 * N, DEPTH),
+            vmem(*plane),
+            vmem(3, *plane),
+            vmem(3, *plane),
+        ),
+        in_specs=[fixed] * 7,
+        out_specs=(whole,) * 10,
+        scratch_shapes=[
             pltpu.VMEM(block, jnp.int32),
+            vmem(3, *plane),
             vmem(3, *plane),
             vmem(3, *plane),
             vmem(3, N, CH, DEPTH),
             vmem(3, 73, CH, DEPTH),
             vmem(73 * N, DEPTH),
-            vmem(25 * N, DEPTH),
             vmem(3 * N, DEPTH),
-            vmem(6, *block),
-            vmem(*block),
-            vmem(*block),
             vmem(25, CH, DEPTH),
-            vmem(*plane),
             vmem(CH, DEPTH),
-            vmem(5, *plane),
-            vmem(5, *plane),
-            vmem(5, *plane),
-            vmem(5, *plane),
-            vmem(3, *plane),
+            vmem(4, *plane),
+            vmem(4, *plane),
+            vmem(4, *plane),
+            vmem(4, *plane),
             pltpu.SMEM((8,), F32),
             pltpu.SMEM((8,), F32),
             pltpu.SMEM((8,), F32),
@@ -454,15 +490,25 @@
             pltpu.SemaphoreType.DMA((COPIES,)),
         ],
         compiler_params=pltpu.CompilerParams(
-            collective_id=0, has_side_effects=True, vmem_limit_bytes=40 * 1024 * 1024
+            collective_id=0, has_side_effects=True, vmem_limit_bytes=24 * 1024 * 1024
         ),
     )(*(hold(a) for a in (displacement, velocity, history, zone, zone_modulus, zone_threshold, zone_density)))
     return pl.pallas_call(
-        store,
-        out_shape=tuple(jax.ShapeDtypeStruct(r.shape, F32) for r in results),
-        in_specs=[whole] * 3,
+        finish,
+        out_shape=(
+            jax.ShapeDtypeStruct((3, *block), F32),
+            jax.ShapeDtypeStruct((3, *block), F32),
+            jax.ShapeDtypeStruct(block, F32),
+        ),
+        in_specs=[whole] * 10,
         out_specs=(fixed,) * 3,
-        scratch_shapes=[pltpu.SemaphoreType.DMA((3,))],
+        scratch_shapes=[
+            vmem(3, *block),
+            vmem(3, *block),
+            vmem(*block),
+            pltpu.SemaphoreType.DMA((3 * PARTS,)),
+        ],
+        compiler_params=pltpu.CompilerParams(vmem_limit_bytes=24 * 1024 * 1024),
     )(*(pltpu.with_memory_space_constraint(r, pltpu.VMEM) for r in results))
 
 

time: 46.6 us -> 45.1 us (0.968)
  the two profiles are of different devices: /device:TPU:59 before, /device:TPU:167 now
where the time goes in v4:
time: 45.1 us; the launch traced here: 45 us
  Pallas kernels  44.4 us (98%)
  between operations  0.64 us (1%)
    pallas_call x1, Pallas kernels, body(): pl.pallas_call(functools.partial(kernel, ngx, ngy), out_shape=(vmem(3, N...  42.8 us
    pallas_call x1, Pallas kernels, body(): pl.pallas_call(finish, out_shape=(jax.ShapeDtypeStruct((3, *block), F32),...  1.6 us

profile of v4, /device:TPU:167, one launch (start us, length us, event | category | flops | bytes accessed | tf_op | source)
XLA Modules:
  0.0 45.0 jit_solution(907853007436039642)
XLA Ops:
  0.6 42.8 %shard_map.94 = (f32[3,25,32,128]{3,2,1,0:T(8,128)S(1)}, f32[3,24,24,128]{3,2,1,0:T(8,128)S(1)}, f32[24,24,128]{2,1,0:T(8,128)S(1)}, f32[6,24,24,128]{3,2,1,0:T(...) custom-call(f32[3,24,24,128]{3,2,1,0:T(8,128)} %disp.1, ...), custom_call_target="tpu_custom_call" | custom-call | tf_op jit(solution)/shard_map/pallas_call | solution.py:454
  43.4 1.6 %shard_map.95 = (f32[3,24,24,128]{3,2,1,0:T(8,128)}, f32[3,24,24,128]{3,2,1,0:T(8,128)}, f32[24,24,128]{2,1,0:T(8,128)}) custom-call(f32[3,25,32,128]{3,2,1,0:T(8,128)S(1)} %get-tuple-element.13.de, f32[3,24,24,128]{3,2,1,0:T(8,128)S(1)} %get-tuple-element.14.v, f32[24,24,128]{2,1,0:T(8,128)S(1)} %get-tuple-element.15.h, ...), custom_call_target="tpu_custom_call" | custom-call | tf_op jit(solution)/shard_map/pallas_call | solution.py:496

commit v5 on v4

--- a/solution.py
+++ b/solution.py
@@ -320,6 +320,7 @@
     for k, source in enumerate((1, 3, 4)):
         pys[k] = scale * u[source, 0:N, N - 1, :]
     pys[3] = jnp.maximum(h[0:N, N - 1, :], limit)
+    start_near(face_x)
 
     nothing = zeros((1, CH, DEPTH))
 
@@ -340,8 +341,8 @@
             yb[pl.ds((25 + c * CH) * N + i, CH, stride=N), :] = middle[i + 1]
         for k in part_y[c]:
             start(k)
-    start(face_x)
     start(face_y)
+    start_far(face_x)
     start(edge_y[0])
     arrived(last_x[2])
     for c in range(3):
@@ -349,32 +350,32 @@
     start(edge_y[1])
     start(edge_y[2])
 
-    def gather(first, number, fresh):
+    def gather(blocks, fresh):
         def group(g, carry):
             off = pl.multiple_of(g * CH, CH)
-            source = jnp.stack([yb[pl.ds((first + k) * N + off, CH), :] for k in range(number)])
             if fresh:
                 total = jnp.zeros((25, CH, DEPTH), F32)
             else:
                 total = jnp.stack([out[pl.ds(m * N + off, CH), :] for m in range(25)])
-            for t in range(TAPS):
-                lo, hi = max(0, first - t), min(25, first + number - t)
-                if lo < hi:
-                    part = total[lo:hi] + WEIGHT[t] * source[lo + t - first : hi + t - first]
-                    pieces = [total[:lo]] * (lo > 0) + [part] + [total[hi:]] * (hi < 25)
-                    total = jnp.concatenate(pieces) if len(pieces) > 1 else part
+            for first, number in blocks:
+                source = jnp.stack([yb[pl.ds((first + k) * N + off, CH), :] for k in range(number)])
+                for t in range(TAPS):
+                    lo, hi = max(0, first - t), min(25, first + number - t)
+                    if lo < hi:
+                        part = total[lo:hi] + WEIGHT[t] * source[lo + t - first : hi + t - first]
+                        pieces = [total[:lo]] * (lo > 0) + [part] + [total[hi:]] * (hi < 25)
+                        total = jnp.concatenate(pieces) if len(pieces) > 1 else part
             for m in range(25):
                 out[pl.ds(m * N + off, CH), :] = total[m]
             return carry
 
-        lax.fori_loop(0, N // CH, group, 0)
-
-    gather(25, N, True)
+        lax.fori_loop(0, N // CH, group, 0, unroll=not fresh)
+
+    gather([(25, N)], True)
     for c in range(3):
         for k in part_y[c]:
             arrived(k)
-        gather(1 + c * CH, CH, False)
-        gather(49 + c * CH, CH, False)
+        gather([(1 + c * CH, CH), (49 + c * CH, CH)], False)
     for k in edge_y:
         arrived(k)
     out[0:N] += WEIGHT[0] * yb[0:N]
@@ -400,7 +401,7 @@
         left(k)
 
 
-PARTS = 4
+PARTS = 6
 
 
 def finish(de, v, h, u, tm, rm, out, iy, sx0, pyi, nd_out, nv_out, nh_out, nd, nv, nh, sem):
@@ -460,7 +461,7 @@
             vmem(6, *block),
             vmem(*block),
             vmem(*block),
-            vmem(25 * N, DEPTH),
+            vmem(26 * N, DEPTH),
             vmem(*plane),
             vmem(3, *plane),
             vmem(3, *plane),

time: 45.1 us -> 45 us (level)
  the two profiles are of different devices: /device:TPU:167 before, /device:TPU:37 now
where the time goes in v5:
time: 45 us; the launch traced here: 44.9 us
  Pallas kernels  44.2 us (98%)
  between operations  0.64 us (1%)
    pallas_call x1, Pallas kernels, body(): pl.pallas_call(functools.partial(kernel, ngx, ngy), out_shape=(vmem(3, N...  42.7 us
    pallas_call x1, Pallas kernels, body(): pl.pallas_call(finish, out_shape=(jax.ShapeDtypeStruct((3, *block), F32),...  1.6 us

profile of v5, /device:TPU:37, one launch (start us, length us, event | category | flops | bytes accessed | tf_op | source)
XLA Modules:
  0.0 44.9 jit_solution(2742366274497278348)
XLA Ops:
  0.6 42.7 %shard_map.94 = (f32[3,25,32,128]{3,2,1,0:T(8,128)S(1)}, f32[3,24,24,128]{3,2,1,0:T(8,128)S(1)}, f32[24,24,128]{2,1,0:T(8,128)S(1)}, f32[6,24,24,128]{3,2,1,0:T(...) custom-call(f32[3,24,24,128]{3,2,1,0:T(8,128)} %disp.1, ...), custom_call_target="tpu_custom_call" | custom-call | tf_op jit(solution)/shard_map/pallas_call | solution.py:455
  43.3 1.6 %shard_map.95 = (f32[3,24,24,128]{3,2,1,0:T(8,128)}, f32[3,24,24,128]{3,2,1,0:T(8,128)}, f32[24,24,128]{2,1,0:T(8,128)}) custom-call(f32[3,25,32,128]{3,2,1,0:T(8,128)S(1)} %get-tuple-element.13.de, f32[3,24,24,128]{3,2,1,0:T(8,128)S(1)} %get-tuple-element.14.v, f32[24,24,128]{2,1,0:T(8,128)S(1)} %get-tuple-element.15.h, ...), custom_call_target="tpu_custom_call" | custom-call | tf_op jit(solution)/shard_map/pallas_call | solution.py:497
